TPU v7x, 256 devices: a whole 4x4x8 slice. The times are simulated.
256 devices in a mesh: rows: 64 (over y, z, core), feat: 4 (over x).
Axes of the slice: x: 4, y: 4, z: 8, core: 2. Of those that a mesh axis runs over, the one named last changes fastest.
Arguments:
- gradients: bfloat16 [32768, 128], P('rows'), may hold values from -6 to 6
- hessians: bfloat16 [32768], P('rows'), may hold values from 0.25 to 2
- bin_words: int32 [128, 32768], P('feat', 'rows'), may hold values from 0 to 4095, as said below
- children: int32 [3, 32768], P(None, 'rows'), may hold values from 0 to 1, as said below
- split_feature: int32 [14], replicated, may hold values from 0 to 255
- split_bin: int32 [14], replicated, may hold values from 0 to 62
Outputs:
- split_gain_one: float32 [128, 256], P('rows', 'feat')
- split_gain_two: float32 [256, 256], P('rows', 'feat')
- split_gain_three: float32 [512, 256], P('rows', 'feat')
- child_scores: float32 [3, 64, 2, 128], P(None, 'rows')
Inputs may be any that keep to these rules, and one draw needn't show every extreme that they name: `children`: of the 512 rows of one device, at most 3 / 4, 1 / 2 and 1 / 4 of 512 lie in one node at depths 1, 2 and 3; every device reaches each of these bounds in some node. `bin_words`: word w of panel p, six bits a feature with the lowest bits first, holds the bins of the panel's features 2 w and 2 w + 1, numbered within the panel of 64 features; slots past the panel's last feature are zero. Every bin is below 64.
All inputs are finite; a program needn't handle non-finite values.
Results may differ from a plain program's by a relative error of at most 0.0003.
Values may be sent and summed in bfloat16 or wider, within the bound.
A program may use at most 64 MiB of HBM per device.

v0:
```python
import jax
import jax.numpy as jnp
from jax import lax
from jax.sharding import PartitionSpec as P

FEATURES = 256
BINS = 64
OUT = 128
LEVELS = 3
penalty = 1.0


def as_sent(array):
    return jax.tree.map(lambda a: a.astype(jnp.bfloat16) if a.dtype == jnp.float32 else a, array)


def swapped(block, axis, stride):
    count = lax.axis_size(axis)
    route = []
    for low in range(count):
        high = low | 1 << stride
        if high != low and high < count:
            route += [(low, high), (high, low)]
    return lax.ppermute(block, axis, route)


def unpack_codes(packed):
    shifts = 6 * jnp.arange(2, dtype=jnp.int32)
    pieces = jnp.bitwise_and(jnp.right_shift(packed[:, None, :], shifts[None, :, None]), 63)
    return pieces.reshape(-1, packed.shape[-1])


def split_terms(cumulative, hess_cum):
    total_sum = cumulative[..., -1:, :]
    hess_total = hess_cum[..., -1:]
    right_sum = total_sum - cumulative
    hess_right = hess_total - hess_cum
    split_score = (
        jnp.sum(cumulative * cumulative, -1) / (hess_cum + penalty)
        + jnp.sum(right_sum * right_sum, -1) / (hess_right + penalty)
        - jnp.sum(total_sum * total_sum, -1) / (hess_total + penalty)
    ) / OUT
    return (split_score, right_sum, hess_right)


def front_index(marked, slot_total):
    running = jnp.cumsum(marked.astype(jnp.int32))
    wanted = jnp.arange(slot_total, dtype=jnp.int32) + 1
    source = jnp.searchsorted(running, wanted, side="left")
    filled = wanted <= running[-1]
    return (jnp.minimum(source, marked.shape[0] - 1), filled)


def pick_rows(values, source, filled):
    taken = jnp.take(values, source, axis=0)
    return jnp.where(filled[:, None], taken, jnp.zeros_like(taken))


def pick_slots(values, source, filled):
    taken = jnp.take(values, source, axis=0)
    return jnp.where(filled, taken, jnp.zeros_like(taken))


def pick_columns(values, source, filled):
    taken = jnp.take(values, source, axis=1)
    return jnp.where(filled[None, :], taken, jnp.zeros_like(taken))


def build_hist(bin_codes, grad_rows, hess_rows, block_rows):
    feat_count = bin_codes.shape[0]
    bin_levels = jnp.arange(BINS, dtype=jnp.int32)

    def add_block(step_index, running):
        start_row = step_index * block_rows
        code_block = lax.dynamic_slice_in_dim(bin_codes, start_row, block_rows, 1)
        grad_block = lax.dynamic_slice_in_dim(grad_rows, start_row, block_rows, 0)
        hess_block = lax.dynamic_slice_in_dim(hess_rows, start_row, block_rows, 0)
        one_hot = (code_block[:, None, :] == bin_levels[None, :, None]).astype(jnp.bfloat16)
        one_hot = one_hot.reshape(feat_count * BINS, block_rows)
        return (
            running[0] + jnp.dot(one_hot, grad_block, preferred_element_type=jnp.float32),
            running[1] + jnp.dot(one_hot, hess_block, preferred_element_type=jnp.float32),
        )

    initial = (
        jnp.zeros((feat_count * BINS, OUT), jnp.float32),
        jnp.zeros((feat_count * BINS,), jnp.float32),
    )
    return lax.fori_loop(0, grad_rows.shape[0] // block_rows, add_block, initial)


def on_device(gradients, hessians, bin_words, children, split_feature, split_bin):
    row_count = lax.axis_size("rows")
    top_bit = row_count.bit_length() - 1
    row_index = lax.axis_index("rows")
    panel_index = lax.axis_index("feat")
    feat_dev = FEATURES // lax.axis_size("feat")
    row_dev = gradients.shape[0]
    slot_count = 2 * row_dev
    block_rows = min(256, slot_count)
    pad_rows = slot_count - row_dev
    grad_rows = jnp.concatenate([gradients, jnp.zeros((pad_rows, OUT), jnp.bfloat16)], 0)
    hess_rows = jnp.concatenate([hessians, jnp.zeros((pad_rows,), jnp.bfloat16)], 0)
    word_rows = jnp.concatenate(
        [bin_words, jnp.zeros((bin_words.shape[0], pad_rows), jnp.int32)], 1
    )
    child_rows = jnp.concatenate([children, jnp.zeros((children.shape[0], pad_rows), jnp.int32)], 1)
    splits_total = split_feature.shape[0]
    collected = jnp.zeros((splits_total, 2, OUT), jnp.float32)
    gain_list = []
    slot_list = []
    for level_index in range(LEVELS):
        cross_bit = top_bit - 1 - level_index
        half_bit = jnp.bitwise_and(jnp.right_shift(row_index, cross_bit), 1)
        living = hess_rows > 0
        staying = living & (child_rows[level_index] == half_bit)
        leaving = living & (child_rows[level_index] != half_bit)
        sent_hess = jnp.where(leaving, hess_rows, jnp.zeros_like(hess_rows))
        got_grad, got_hess, got_words, got_child = (
            swapped(grad_rows, "rows", cross_bit),
            swapped(sent_hess, "rows", cross_bit),
            swapped(as_sent(word_rows), "rows", cross_bit).astype(word_rows.dtype),
            swapped(as_sent(child_rows), "rows", cross_bit).astype(child_rows.dtype),
        )
        accepted = jnp.concatenate([staying, got_hess > 0])
        source, filled = front_index(accepted, slot_count)
        grad_rows = pick_rows(jnp.concatenate([grad_rows, got_grad], 0), source, filled)
        hess_rows = pick_slots(jnp.concatenate([hess_rows, got_hess], 0), source, filled)
        word_rows = pick_columns(jnp.concatenate([word_rows, got_words], 1), source, filled)
        child_rows = pick_columns(jnp.concatenate([child_rows, got_child], 1), source, filled)
        bin_codes = unpack_codes(word_rows)
        hist_grad, hist_hess = build_hist(bin_codes, grad_rows, hess_rows, block_rows)
        group_size = row_count >> level_index + 1
        node_count = 2 ** (level_index + 1)
        node_here = jnp.right_shift(row_index, top_bit - level_index - 1)
        share_grad = hist_grad.reshape(feat_dev, BINS * OUT)
        share_hess = hist_hess.reshape(feat_dev, BINS)
        for step_bit in reversed(range(top_bit - level_index - 1)):
            half_rows = share_grad.shape[0] // 2
            upper_half = jnp.bitwise_and(jnp.right_shift(row_index, step_bit), 1) == 1
            keep_grad = jnp.where(upper_half, share_grad[half_rows:], share_grad[:half_rows])
            give_grad = jnp.where(upper_half, share_grad[:half_rows], share_grad[half_rows:])
            keep_hess = jnp.where(upper_half, share_hess[half_rows:], share_hess[:half_rows])
            give_hess = jnp.where(upper_half, share_hess[:half_rows], share_hess[half_rows:])
            got_partial, got_curv = swapped((give_grad, give_hess), "rows", step_bit)
            share_grad = keep_grad + got_partial
            share_hess = keep_hess + got_curv
        share_count = share_grad.shape[0]
        cumulative = jnp.cumsum(share_grad.reshape(share_count, BINS, OUT), axis=1)
        hess_cum = jnp.cumsum(share_hess, axis=1)
        split_score, right_sum, hess_right = split_terms(cumulative, hess_cum)
        gain_list.append(split_score)
        position = jnp.bitwise_and(row_index, group_size - 1)
        split_slot = node_count - 2 + node_here
        feature_id = split_feature[split_slot]
        bin_id = split_bin[split_slot]
        inner_feature = feature_id % feat_dev
        is_owner = (feature_id // feat_dev == panel_index) & (
            inner_feature // share_count == position
        )
        chosen = (
            (jnp.arange(share_count)[:, None] == inner_feature % share_count)
            & (jnp.arange(BINS)[None, :] == bin_id)
            & is_owner
        )
        left_grad = jnp.sum(jnp.where(chosen[..., None], cumulative, 0.0), axis=(0, 1))
        left_hess = jnp.sum(jnp.where(chosen, hess_cum, 0.0))
        right_grad = jnp.sum(jnp.where(chosen[..., None], right_sum, 0.0), axis=(0, 1))
        right_hess = jnp.sum(jnp.where(chosen, hess_right, 0.0))
        child_pair = jnp.stack(
            [
                -left_grad / jnp.sqrt(left_hess + penalty),
                -right_grad / jnp.sqrt(right_hess + penalty),
            ],
            0,
        )
        slot_match = jnp.arange(splits_total) == split_slot
        collected = collected + jnp.where(slot_match[:, None, None], child_pair[None], 0.0)
        slot_list.append(split_slot)
    totals = lax.psum(collected, ("rows", "feat"))
    child_scores = jnp.stack([totals[slot_index] for slot_index in slot_list], 0)[:, None]
    return (gain_list[0], gain_list[1], gain_list[2], child_scores)


def solution(mesh):
    placed = (P("rows", None), P("rows"), P("feat", "rows"), P(None, "rows"), P(), P())
    return jax.shard_map(
        on_device,
        mesh=mesh,
        in_specs=placed,
        out_specs=(
            P("rows", "feat"),
            P("rows", "feat"),
            P("rows", "feat"),
            P(None, "rows", None, None),
        ),
        check_vma=False,
    )
```

profile of v0, /device:TPU:1, one launch (start us, length us, event | category | flops | bytes accessed | tf_op | source)
XLA Modules:
  0.0 707.1 jit_solution(15301522432196689266)
XLA Ops:
  2.1 3.7 collective-permute-start
  22.0 74.8 %while.98 = (s32[]{:T(128)}, u32[1024]{0:T(1024)S(1)}, u32[1024]{0:T(1024)S(1)}, s32[2048]{0:T(1024)S(1)}, s32[]{:T(128)}, /*index=5*/s32[]{:T(128)}, s32[]{}) while((s32[]{:T(128)}, u32[1024]{0:T(1024)S(1)}, u32[1024]{0:T(1024)S(1)}, s32[2048]{0:T(1024)S(1)}, s32[]{:T(128)}, /*index=5*/s32[]{:T(128)}, s32[]{}) %tuple.223), condition=%wide.region_3.4_spmd.clone, body=%wide.region_2.3_spmd.clone.sunk | while | flops 20484 | bytes 63589 | solution.py:49
  22.0 6.2 gather_fusion
  28.3 6.2 gather_fusion
  34.5 6.2 gather_fusion
  40.7 6.2 gather_fusion
  47.0 6.2 gather_fusion
  53.2 6.2 gather_fusion
  59.4 6.2 gather_fusion
  65.7 6.2 gather_fusion
  71.9 6.2 gather_fusion
  78.1 6.2 gather_fusion
  84.4 6.2 gather_fusion
  90.6 6.2 gather_fusion
  97.5 6.8 gather_fusion.5
  112.2 74.8 %while.100 = (s32[]{:T(128)}, u32[1024]{0:T(1024)S(1)}, u32[1024]{0:T(1024)S(1)}, s32[2048]{0:T(1024)S(1)}, s32[]{:T(128)}, /*index=5*/s32[]{:T(128)}, s32[]{}) while((s32[]{:T(128)}, u32[1024]{0:T(1024)S(1)}, u32[1024]{0:T(1024)S(1)}, s32[2048]{0:T(1024)S(1)}, s32[]{:T(128)}, /*index=5*/s32[]{:T(128)}, s32[]{}) %tuple.226), condition=%wide.region_14.19_spmd.clone, body=%wide.region_13.18_spmd.clone.sunk | while | flops 20484 | bytes 63589 | solution.py:49
  112.2 6.2 gather_fusion.1
  118.5 6.2 gather_fusion.1
  124.7 6.2 gather_fusion.1
  131.0 6.2 gather_fusion.1
  137.2 6.2 gather_fusion.1
  143.4 6.2 gather_fusion.1
  149.7 6.2 gather_fusion.1
  155.9 6.2 gather_fusion.1
  162.1 6.2 gather_fusion.1
  168.4 6.2 gather_fusion.1
  174.6 6.2 gather_fusion.1
  180.8 6.2 gather_fusion.1
  188.3 6.8 gather_fusion.9
  199.6 7.0 collective-permute-start.26
  210.8 74.8 %while.102 = (s32[]{:T(128)}, u32[1024]{0:T(1024)S(1)}, u32[1024]{0:T(1024)S(1)}, s32[2048]{0:T(1024)S(1)}, s32[]{:T(128)}, /*index=5*/s32[]{:T(128)}, s32[]{}) while((s32[]{:T(128)}, u32[1024]{0:T(1024)S(1)}, u32[1024]{0:T(1024)S(1)}, s32[2048]{0:T(1024)S(1)}, s32[]{:T(128)}, /*index=5*/s32[]{:T(128)}, s32[]{}) %tuple.229), condition=%wide.region_25.30_spmd.clone, body=%wide.region_24.29_spmd.clone.sunk | while | flops 20484 | bytes 63589 | solution.py:49
  210.8 6.2 gather_fusion.2
  217.0 6.2 gather_fusion.2
  223.3 6.2 gather_fusion.2
  229.5 6.2 gather_fusion.2
  235.7 6.2 gather_fusion.2
  242.0 6.2 gather_fusion.2
  248.2 6.2 gather_fusion.2
  254.4 6.2 gather_fusion.2
  260.7 6.2 gather_fusion.2
  266.9 6.2 gather_fusion.2
  273.2 6.2 gather_fusion.2
  279.4 6.2 gather_fusion.2
  286.2 6.8 gather_fusion.13
  293.4 4.0 gather_fusion.3
  303.2 6.0 collective-permute-done.15
  311.3 4.1 gather_fusion.7
  320.3 4.3 gather_fusion.4
  325.9 10.0 %collective-permute-done.27 = s32[32,1024]{0,1:T(8,128)} collective-permute-done((s32[32,1024]{0,1:T(8,128)S(1)}, s32[32,1024]{0,1:T(8,128)}, u32[]{:S(2)}, u32[]{:S(2)}) %collective-permute-start.27) | collective-permute-done | bytes 131104 | tf_op jit(solution)/shard_map/ppermute | solution.py:24
  338.0 5.3 gather_fusion.11
  347.7 14.4 %while.99 = (s32[]{:T(128)}, f32[4096,128]{1,0:T(8,128)S(1)}, f32[4096]{0:T(1024)S(1)}, s32[64,1024]{1,0:T(8,128)}, bf16[1024,128]{1,0:T(8,128)(2,1)S(1)}, /*ind...) while((s32[]{:T(128)}, f32[4096,128]{1,0:T(8,128)S(1)}, ...), condition=%wide.region_5.9_spmd.clone, body=%wide.region_4.8_spmd.clone.sunk | while | flops 272637952 | bytes 7735978 | solution.py:89
  371.3 8.6 %collective-permute-start.10 = (f32[8,64]{1,0:T(8,128)S(1)}, f32[8,64]{1,0:T(8,128)S(1)}, u32[]{:S(2)}, u32[]{:S(2)}) collective-permute-start(f32[8,64]{1,0:T(8,128)S(1)} %slice_select_fusion.26), channel_id=1, source_target_pairs={{0,16},{16,0},{4,20},{20,4},{8,24},{24,8},{12,28},{28,12},{32,48},... | collective-permute-start | bytes 6152 | tf_op jit(solution)/shard_map/ppermute | solution.py:24
  395.3 22.7 %while.101 = (s32[]{:T(128)}, f32[4096,128]{1,0:T(8,128)}, f32[4096]{0:T(1024)S(1)}, s32[64,1024]{1,0:T(8,128)}, bf16[1024,128]{1,0:T(8,128)(2,1)S(1)}, /*index=...) while((s32[]{:T(128)}, f32[4096,128]{1,0:T(8,128)}, ...), condition=%wide.region_16.21_spmd.clone, body=%wide.region_15.20_spmd.clone.sunk | while | flops 272637952 | bytes 7735978 | solution.py:89
  401.4 3.7 convolution_add_fusion.7
  420.2 6.4 collective-permute-start.12
  448.5 17.1 %while.103 = (s32[]{:T(128)}, f32[4096,128]{1,0:T(8,128)S(1)}, f32[4096]{0:T(1024)S(1)}, s32[64,1024]{1,0:T(8,128)}, bf16[1024,128]{1,0:T(8,128)(2,1)S(1)}, /*in...) while((s32[]{:T(128)}, f32[4096,128]{1,0:T(8,128)S(1)}, ...), condition=%wide.region_27.32_spmd.clone, body=%wide.region_26.31_spmd.clone.sunk | while | flops 272637952 | bytes 7735978 | solution.py:89
  465.8 7.1 %collective-permute-start.24 = (f32[4,64]{1,0:T(4,128)S(1)}, f32[4,64]{1,0:T(4,128)S(1)}, u32[]{:S(2)}, u32[]{:S(2)}) collective-permute-start(f32[4,64]{1,0:T(4,128)S(1)} %slice_select_fusion.27), channel_id=1, source_target_pairs={{0,4},{4,0},{8,12},{12,8},{16,20},{20,16},{24,28},{28,24},{32,36},... | collective-permute-start | bytes 3080 | tf_op jit(solution)/shard_map/ppermute | solution.py:24
  472.9 18.8 %collective-permute-done.32 = f32[32,64]{1,0:T(8,128)S(1)} collective-permute-done((f32[32,64]{1,0:T(8,128)S(1)}, f32[32,64]{1,0:T(8,128)S(1)}, u32[]{:S(2)}, u32[]{:S(2)}) %collective-permute-start.32) | collective-permute-done | bytes 8224 | tf_op jit(solution)/shard_map/ppermute | solution.py:24
  508.4 73.3 %collective-permute-done.29 = f32[32,8192]{1,0:T(8,128)} collective-permute-done((f32[32,8192]{1,0:T(8,128)}, f32[32,8192]{1,0:T(8,128)}, u32[]{:S(2)}, u32[]{:S(2)}) %collective-permute-start.29) | collective-permute-done | bytes 1048608 | tf_op jit(solution)/shard_map/ppermute | solution.py:24
  585.3 7.6 %collective-permute-done.18 = f32[16,8192]{1,0:T(8,128)S(1)} collective-permute-done((f32[16,8192]{1,0:T(8,128)S(1)}, f32[16,8192]{1,0:T(8,128)S(1)}, u32[]{:S(2)}, u32[]{:S(2)}) %collective-permute-start.18) | collective-permute-done | bytes 524320 | tf_op jit(solution)/shard_map/ppermute | solution.py:24
  592.9 11.2 %collective-permute-done.5 = f32[8,8192]{1,0:T(8,128)S(1)} collective-permute-done((f32[8,8192]{1,0:T(8,128)S(1)}, f32[8,8192]{1,0:T(8,128)S(1)}, u32[]{:S(2)}, u32[]{:S(2)}) %collective-permute-start.5) | collective-permute-done | bytes 262176 | tf_op jit(solution)/shard_map/ppermute | solution.py:24
  606.1 6.3 collective-permute-done.6
  613.1 4.9 collective-permute-done.19
  629.2 76.1 %psum.7 = f32[14,2,128]{2,1,0:T(2,128)S(1)} all-reduce(f32[14,2,128]{2,1,0:T(2,128)S(1)} %select_add_fusion.9), channel_id=1, replica_groups=mesh['rows'=64,'feat'=4] {'rows','feat'}, use_global_device_ids=true, to_apply=%region_45.50 | all-reduce | flops 3584 | bytes 28672 | tf_op jit(solution)/shard_map/psum | solution.py:180
  (556 shorter events, 181.2 us)
Async XLA Ops:
  2.1 18.7 %collective-permute-start = (bf16[1024]{0:T(1024)(128)(2,1)S(1)}, bf16[1024]{0:T(1024)(128)(2,1)S(1)}, u32[]{:S(2)}, u32[]{:S(2)}) collective-permute-start(bf16[1024]{0:T(1024)(128)(2,1)S(1)} %and_select_fusion.2), channel_id=1, source_target_pairs={{0,128},{128,0},{4,132},{132,4},{8,136},{136,8},{12,140},{140,12},... | collective-permute-start | bytes 6152 | tf_op jit(solution)/shard_map/ppermute | solution.py:24
  6.6 97.8 %collective-permute-start.13 = (s32[3,1024]{1,0:T(4,128)S(1)}, s32[3,1024]{1,0:T(4,128)S(1)}, u32[]{:S(2)}, u32[]{:S(2)}) collective-permute-start(s32[3,1024]{1,0:T(4,128)S(1)} %concatenate.74), channel_id=1, source_target_pairs={{0,128},{128,0},{4,132},{132,4},{8,136},{136,8},{12,140},{140,12},... | collective-permute-start | bytes 36872 | tf_op jit(solution)/shard_map/ppermute | solution.py:24
  7.4 285.6 %collective-permute-start.1 = (s32[32,1024]{1,0:T(8,128)S(1)}, s32[32,1024]{1,0:T(8,128)S(1)}, u32[]{:S(2)}, u32[]{:S(2)}) collective-permute-start(s32[32,1024]{1,0:T(8,128)S(1)} %concatenate.78), channel_id=1, source_target_pairs={{0,128},{128,0},{4,132},{132,4},{8,136},{136,8},{12,140},{140,12},... | collective-permute-start | bytes 393224 | tf_op jit(solution)/shard_map/ppermute | solution.py:24
  12.1 306.9 %collective-permute-start.2 = (bf16[1024,128]{1,0:T(8,128)(2,1)}, bf16[1024,128]{1,0:T(8,128)(2,1)}, u32[]{:S(2)}, u32[]{:S(2)}) collective-permute-start(bf16[1024,128]{1,0:T(8,128)(2,1)} %concatenate.80), channel_id=1, source_target_pairs={{0,128},{128,0},{4,132},{132,4},{8,136},{136,8},{12,140},{140,12},... | collective-permute-start | bytes 786440 | tf_op jit(solution)/shard_map/ppermute | solution.py:24
  22.0 75.5 %copy-start.8 = (bf16[512]{0:T(512)(128)(2,1)S(1)}, bf16[512]{0:T(512)(128)(2,1)}, u32[]{:S(2)}) copy-start(bf16[512]{0:T(512)(128)(2,1)} %param.27) | copy-start | bytes 3076
  96.8 7.5 %copy-start.7 = (s32[3,512]{1,0:T(4,128)S(1)}, s32[3,512]{1,0:T(4,128)}, u32[]{:S(2)}) copy-start(s32[3,512]{1,0:T(4,128)} %param.29) | copy-start | bytes 18436
  109.1 2.5 collective-permute-start.14
  111.1 84.0 %collective-permute-start.25 = (s32[3,1024]{0,1:T(8,128)S(1)}, s32[3,1024]{0,1:T(8,128)S(1)}, u32[]{:S(2)}, u32[]{:S(2)}) collective-permute-start(s32[3,1024]{0,1:T(8,128)S(1)} %bitcast_select_fusion.2), channel_id=1, source_target_pairs={{0,64},{64,0},{4,68},{68,4},{8,72},{72,8},{12,76},{76,12},{16,80},... | collective-permute-start | bytes 36872 | tf_op jit(solution)/shard_map/ppermute | solution.py:24
  199.6 10.6 %collective-permute-start.26 = (bf16[1024]{0:T(1024)(128)(2,1)S(1)}, bf16[1024]{0:T(1024)(128)(2,1)S(1)}, u32[]{:S(2)}, u32[]{:S(2)}) collective-permute-start(bf16[1024]{0:T(1024)(128)(2,1)S(1)} %and_select_fusion), channel_id=1, source_target_pairs={{0,32},{32,0},{4,36},{36,4},{8,40},{40,8},{12,44},{44,12},{16,48},... | collective-permute-start | bytes 6152 | tf_op jit(solution)/shard_map/ppermute | solution.py:24
  285.6 7.4 %copy-start.6 = (s32[32,512]{1,0:T(8,128)S(1)}, s32[32,512]{1,0:T(8,128)}, u32[]{:S(2)}) copy-start(s32[32,512]{1,0:T(8,128)} %param.28) | copy-start | bytes 196612
  298.8 10.4 %collective-permute-start.15 = (s32[32,1024]{0,1:T(8,128)S(1)}, s32[32,1024]{0,1:T(8,128)}, u32[]{:S(2)}, u32[]{:S(2)}) collective-permute-start(s32[32,1024]{0,1:T(8,128)S(1)} %bitcast_select_fusion.3), channel_id=1, source_target_pairs={{0,64},{64,0},{4,68},{68,4},{8,72},{72,8},{12,76},{76,12},{16,80},... | collective-permute-start | bytes 393224 | tf_op jit(solution)/shard_map/ppermute | solution.py:24
  302.1 41.2 %copy-start.9 = (pred[1024]{0:T(1024)(128)(4,1)}, pred[1024]{0:T(1024)(128)(4,1)S(1)}, u32[]{:S(2)}) copy-start(pred[1024]{0:T(1024)(128)(4,1)S(1)} %fusion.26) | copy-start | bytes 3076
  311.3 7.7 %copy-start.5 = (bf16[512,128]{1,0:T(8,128)(2,1)S(1)}, bf16[512,128]{1,0:T(8,128)(2,1)}, u32[]{:S(2)}) copy-start(bf16[512,128]{1,0:T(8,128)(2,1)} %param.26) | copy-start | bytes 393220
  315.7 20.2 %collective-permute-start.27 = (s32[32,1024]{0,1:T(8,128)S(1)}, s32[32,1024]{0,1:T(8,128)}, u32[]{:S(2)}, u32[]{:S(2)}) collective-permute-start(s32[32,1024]{0,1:T(8,128)S(1)} %bitcast_select_fusion.1), channel_id=1, source_target_pairs={{0,32},{32,0},{4,36},{36,4},{8,40},{40,8},{12,44},{44,12},{16,48},... | collective-permute-start | bytes 393224 | tf_op jit(solution)/shard_map/ppermute | solution.py:24
  338.0 8.7 %copy-start.3 = (s32[64,1024]{1,0:T(8,128)S(1)}, s32[64,1024]{1,0:T(8,128)}, u32[]{:S(2)}) copy-start(s32[64,1024]{1,0:T(8,128)} %shift_right_arithmetic.97) | copy-start | bytes 786436
  338.0 8.7 %copy-start.4 = (s32[64,1024]{1,0:T(8,128)S(1)}, s32[64,1024]{1,0:T(8,128)}, u32[]{:S(2)}) copy-start(s32[64,1024]{1,0:T(8,128)} %shift_right_arithmetic.103) | copy-start | bytes 786436
  338.0 8.7 %copy-start.11 = (s32[64]{0:T(128)S(1)}, s32[64]{0:T(128)}, u32[]{:S(2)}) copy-start(s32[64]{0:T(128)} %shift_right_arithmetic.99) | copy-start | bytes 772
  362.1 5.9 copy-start
  362.2 2.6 collective-permute-start.8
  364.8 6.5 collective-permute-start.9
  371.3 9.9 %collective-permute-start.10 = (f32[8,64]{1,0:T(8,128)S(1)}, f32[8,64]{1,0:T(8,128)S(1)}, u32[]{:S(2)}, u32[]{:S(2)}) collective-permute-start(f32[8,64]{1,0:T(8,128)S(1)} %slice_select_fusion.26), channel_id=1, source_target_pairs={{0,16},{16,0},{4,20},{20,4},{8,24},{24,8},{12,28},{28,12},{32,48},... | collective-permute-start | bytes 6152 | tf_op jit(solution)/shard_map/ppermute | solution.py:24
  379.9 10.8 %collective-permute-start.16 = (bf16[1024,128]{1,0:T(8,128)(2,1)S(1)}, bf16[1024,128]{1,0:T(8,128)(2,1)}, u32[]{:S(2)}, u32[]{:S(2)}) collective-permute-start(bf16[1024,128]{1,0:T(8,128)(2,1)S(1)} %get-tuple-element.1187), channel_id=1, source_target_pairs={{0,64},{64,0},{4,68},{68,4},{8,72},{72,8},{12,76},{76,12},{16,80},... | collective-permute-start | bytes 786440 | tf_op jit(solution)/shard_map/ppermute | solution.py:24
  381.2 9.5 %collective-permute-start.11 = (f32[4,64]{1,0:T(4,128)S(1)}, f32[4,64]{1,0:T(4,128)S(1)}, u32[]{:S(2)}, u32[]{:S(2)}) collective-permute-start(f32[4,64]{1,0:T(4,128)S(1)} %slice_select_fusion.28), channel_id=1, source_target_pairs={{0,8},{8,0},{4,12},{12,4},{16,24},{24,16},{20,28},{28,20},{32,40},... | collective-permute-start | bytes 3080 | tf_op jit(solution)/shard_map/ppermute | solution.py:24
  388.2 112.1 %collective-permute-start.3 = (f32[32,8192]{1,0:T(8,128)}, f32[32,8192]{1,0:T(8,128)}, u32[]{:S(2)}, u32[]{:S(2)}) collective-permute-start(f32[32,8192]{1,0:T(8,128)} %select_n.551), channel_id=1, source_target_pairs={{0,64},{64,0},{4,68},{68,4},{8,72},{72,8},{12,76},{76,12},{16,80},... | collective-permute-start | bytes 3145736 | tf_op jit(solution)/shard_map/ppermute | solution.py:24
  418.1 8.6 %collective-permute-start.21 = (f32[32,64]{1,0:T(8,128)S(1)}, f32[32,64]{1,0:T(8,128)S(1)}, u32[]{:S(2)}, u32[]{:S(2)}) collective-permute-start(f32[32,64]{1,0:T(8,128)S(1)} %select_n.603), channel_id=1, source_target_pairs={{0,32},{32,0},{4,36},{36,4},{8,40},{40,8},{12,44},{44,12},{16,48},... | collective-permute-start | bytes 24584 | tf_op jit(solution)/shard_map/ppermute | solution.py:24
  420.2 7.2 %collective-permute-start.12 = (f32[2,64]{1,0:T(2,128)S(1)}, f32[2,64]{1,0:T(2,128)S(1)}, u32[]{:S(2)}, u32[]{:S(2)}) collective-permute-start(f32[2,64]{1,0:T(2,128)S(1)} %broadcast_select_fusion.1), channel_id=1, source_target_pairs={{0,4},{4,0},{8,12},{12,8},{16,20},{20,16},{24,28},{28,24},{32,36},... | collective-permute-start | bytes 1544 | tf_op jit(solution)/shard_map/ppermute | solution.py:24
  426.7 4.5 collective-permute-start.22
  427.7 16.2 %collective-permute-start.28 = (bf16[1024,128]{1,0:T(8,128)(2,1)S(1)}, bf16[1024,128]{1,0:T(8,128)(2,1)}, u32[]{:S(2)}, u32[]{:S(2)}) collective-permute-start(bf16[1024,128]{1,0:T(8,128)(2,1)S(1)} %get-tuple-element.1189), channel_id=1, source_target_pairs={{0,32},{32,0},{4,36},{36,4},{8,40},{40,8},{12,44},{44,12},{16,48},... | collective-permute-start | bytes 786440 | tf_op jit(solution)/shard_map/ppermute | solution.py:24
  431.2 12.7 %collective-permute-start.23 = (f32[8,64]{1,0:T(8,128)S(1)}, f32[8,64]{1,0:T(8,128)S(1)}, u32[]{:S(2)}, u32[]{:S(2)}) collective-permute-start(f32[8,64]{1,0:T(8,128)S(1)} %slice_select_fusion.25), channel_id=1, source_target_pairs={{0,8},{8,0},{4,12},{12,4},{16,24},{24,16},{20,28},{28,20},{32,40},... | collective-permute-start | bytes 6152 | tf_op jit(solution)/shard_map/ppermute | solution.py:24
  437.7 67.3 %collective-permute-start.17 = (f32[32,8192]{1,0:T(8,128)}, f32[32,8192]{1,0:T(8,128)}, u32[]{:S(2)}, u32[]{:S(2)}) collective-permute-start(f32[32,8192]{1,0:T(8,128)} %select_n.589), channel_id=1, source_target_pairs={{0,32},{32,0},{4,36},{36,4},{8,40},{40,8},{12,44},{44,12},{16,48},... | collective-permute-start | bytes 3145736 | tf_op jit(solution)/shard_map/ppermute | solution.py:24
  440.8 7.4 %copy-start.10 = (pred[1024]{0:T(1024)(128)(4,1)S(1)}, pred[1024]{0:T(1024)(128)(4,1)}, u32[]{:S(2)}) copy-start(pred[1024]{0:T(1024)(128)(4,1)} %copy-done.9) | copy-start | bytes 3076
  465.7 26.0 %collective-permute-start.32 = (f32[32,64]{1,0:T(8,128)S(1)}, f32[32,64]{1,0:T(8,128)S(1)}, u32[]{:S(2)}, u32[]{:S(2)}) collective-permute-start(f32[32,64]{1,0:T(8,128)S(1)} %select_n.632), channel_id=1, source_target_pairs={{0,16},{16,0},{4,20},{20,4},{8,24},{24,8},{12,28},{28,12},{32,48},... | collective-permute-start | bytes 24584 | tf_op jit(solution)/shard_map/ppermute | solution.py:24
  465.8 26.0 %collective-permute-start.24 = (f32[4,64]{1,0:T(4,128)S(1)}, f32[4,64]{1,0:T(4,128)S(1)}, u32[]{:S(2)}, u32[]{:S(2)}) collective-permute-start(f32[4,64]{1,0:T(4,128)S(1)} %slice_select_fusion.27), channel_id=1, source_target_pairs={{0,4},{4,0},{8,12},{12,8},{16,20},{20,16},{24,28},{28,24},{32,36},... | collective-permute-start | bytes 3080 | tf_op jit(solution)/shard_map/ppermute | solution.py:24
  491.7 2.6 collective-permute-start.33
  494.3 5.8 collective-permute-start.34
  496.9 3.4 copy-start.1
  499.5 82.2 %collective-permute-start.29 = (f32[32,8192]{1,0:T(8,128)}, f32[32,8192]{1,0:T(8,128)}, u32[]{:S(2)}, u32[]{:S(2)}) collective-permute-start(f32[32,8192]{1,0:T(8,128)} %select_n.621), channel_id=1, source_target_pairs={{0,16},{16,0},{4,20},{20,4},{8,24},{24,8},{12,28},{28,12},{32,48},... | collective-permute-start | bytes 3145736 | tf_op jit(solution)/shard_map/ppermute | solution.py:24
  500.3 4.7 copy-start.2
  501.8 81.4 %collective-permute-start.4 = (f32[16,8192]{1,0:T(8,128)S(1)}, f32[16,8192]{1,0:T(8,128)S(1)}, u32[]{:S(2)}, u32[]{:S(2)}) collective-permute-start(f32[16,8192]{1,0:T(8,128)S(1)} %slice_select_fusion.9), channel_id=1, source_target_pairs={{0,32},{32,0},{4,36},{36,4},{8,40},{40,8},{12,44},{44,12},{16,48},... | collective-permute-start | bytes 1572872 | tf_op jit(solution)/shard_map/ppermute | solution.py:24
  506.4 86.4 %collective-permute-start.18 = (f32[16,8192]{1,0:T(8,128)S(1)}, f32[16,8192]{1,0:T(8,128)S(1)}, u32[]{:S(2)}, u32[]{:S(2)}) collective-permute-start(f32[16,8192]{1,0:T(8,128)S(1)} %slice_select_fusion.8), channel_id=1, source_target_pairs={{0,16},{16,0},{4,20},{20,4},{8,24},{24,8},{12,28},{28,12},{32,48},... | collective-permute-start | bytes 1572872 | tf_op jit(solution)/shard_map/ppermute | solution.py:24
  583.0 35.7 %collective-permute-start.30 = (f32[16,8192]{1,0:T(8,128)S(1)}, f32[16,8192]{1,0:T(8,128)S(1)}, u32[]{:S(2)}, u32[]{:S(2)}) collective-permute-start(f32[16,8192]{1,0:T(8,128)S(1)} %slice_select_fusion.7), channel_id=1, source_target_pairs={{0,8},{8,0},{4,12},{12,4},{16,24},{24,16},{20,28},{28,20},{32,40},... | collective-permute-start | bytes 1572872 | tf_op jit(solution)/shard_map/ppermute | solution.py:24
  583.3 20.8 %collective-permute-start.5 = (f32[8,8192]{1,0:T(8,128)S(1)}, f32[8,8192]{1,0:T(8,128)S(1)}, u32[]{:S(2)}, u32[]{:S(2)}) collective-permute-start(f32[8,8192]{1,0:T(8,128)S(1)} %slice_select_fusion.12), channel_id=1, source_target_pairs={{0,16},{16,0},{4,20},{20,4},{8,24},{24,8},{12,28},{28,12},{32,48},... | collective-permute-start | bytes 786440 | tf_op jit(solution)/shard_map/ppermute | solution.py:24
  604.2 8.2 %collective-permute-start.6 = (f32[4,8192]{1,0:T(4,128)S(1)}, f32[4,8192]{1,0:T(4,128)S(1)}, u32[]{:S(2)}, u32[]{:S(2)}) collective-permute-start(f32[4,8192]{1,0:T(4,128)S(1)} %slice_select_fusion.14), channel_id=1, source_target_pairs={{0,8},{8,0},{4,12},{12,4},{16,24},{24,16},{20,28},{28,20},{32,40},... | collective-permute-start | bytes 393224 | tf_op jit(solution)/shard_map/ppermute | solution.py:24
  604.6 13.4 %collective-permute-start.19 = (f32[8,8192]{1,0:T(8,128)S(1)}, f32[8,8192]{1,0:T(8,128)S(1)}, u32[]{:S(2)}, u32[]{:S(2)}) collective-permute-start(f32[8,8192]{1,0:T(8,128)S(1)} %slice_select_fusion.11), channel_id=1, source_target_pairs={{0,8},{8,0},{4,12},{12,4},{16,24},{24,16},{20,28},{28,20},{32,40},... | collective-permute-start | bytes 786440 | tf_op jit(solution)/shard_map/ppermute | solution.py:24
  612.5 6.5 collective-permute-start.7
  618.1 1.5 copy-start.15
  618.1 1.5 copy-start.16
  618.1 5.0 copy-start.19
  618.1 5.0 copy-start.20
  618.1 4.3 collective-permute-start.20
  618.8 7.8 %copy-start.17 = (pred[8]{0:T(512)(128)(4,1)S(1)}, pred[8]{0:T(512)(128)(4,1)}, u32[]{:S(2)}) copy-start(pred[8]{0:T(512)(128)(4,1)} %iota_compare_fusion.1) | copy-start | bytes 28
  618.8 7.8 %copy-start.18 = (pred[64]{0:T(512)(128)(4,1)S(1)}, pred[64]{0:T(512)(128)(4,1)}, u32[]{:S(2)}) copy-start(pred[64]{0:T(512)(128)(4,1)} %iota_compare_fusion) | copy-start | bytes 196
  618.8 10.3 %copy-start.12 = (pred[14]{0:T(512)(128)(4,1)S(1)}, pred[14]{0:T(512)(128)(4,1)}, u32[]{:S(2)}) copy-start(pred[14]{0:T(512)(128)(4,1)} %get-tuple-element.829) | copy-start | bytes 46
  618.8 10.3 %copy-start.13 = (pred[14]{0:T(512)(128)(4,1)S(1)}, pred[14]{0:T(512)(128)(4,1)}, u32[]{:S(2)}) copy-start(pred[14]{0:T(512)(128)(4,1)} %get-tuple-element.830) | copy-start | bytes 46
  618.8 10.3 %copy-start.14 = (pred[14]{0:T(512)(128)(4,1)S(1)}, pred[14]{0:T(512)(128)(4,1)}, u32[]{:S(2)}) copy-start(pred[14]{0:T(512)(128)(4,1)} %iota_compare_fusion.2) | copy-start | bytes 46
  618.9 7.2 %collective-permute-start.31 = (f32[8,8192]{1,0:T(8,128)S(1)}, f32[8,8192]{1,0:T(8,128)S(1)}, u32[]{:S(2)}, u32[]{:S(2)}) collective-permute-start(f32[8,8192]{1,0:T(8,128)S(1)} %slice_select_fusion.10), channel_id=1, source_target_pairs={{0,4},{4,0},{8,12},{12,8},{16,20},{20,16},{24,28},{28,24},{32,36},... | collective-permute-start | bytes 786440 | tf_op jit(solution)/shard_map/ppermute | solution.py:24
where the time goes:
time: 718 us; the launch traced here: 707 us
  local copies, waits for them, and re-layouts  310 us (43%)
  waiting for transfers between devices  148 us (21%)
  blocking collectives  76.1 us (11%)
  starting transfers between devices  69.2 us (10%)
  other arithmetic  58 us (8%)
  matrix products  30.3 us (4%)
  between operations  13.7 us (2%)
    gather x36, local copies, waits for them, and re-layouts, front_index(): source = jnp.searchsorted(running, wanted, side='left')  222 us
    ppermute x35, waiting for transfers between devices, swapped(): return lax.ppermute(block, axis, route)  148 us
    psum x1, blocking collectives, on_device(): totals = lax.psum(collected, ('rows', 'feat'))  76.1 us
    ppermute x35, starting transfers between devices, swapped(): return lax.ppermute(block, axis, route)  69.2 us
    dot_general x12, matrix products, add_block(): jnp.dot(one_hot, grad_block, preferred_element_type=jnp.float32)  22.6 us
    gather x3, local copies, waits for them, and re-layouts, pick_slots(): taken = jnp.take(values, source, axis=0)  20.4 us
    gather x5, local copies, waits for them, and re-layouts, pick_columns(): taken = jnp.take(values, source, axis=1)  19 us
  transfers between devices with their start and end apart: 35, of which 14 were waited for; matrix products, arithmetic and copies ran while one was open for 52% of the time, Pallas kernels for 0%

commit v1 on v0

--- a/solution.py
+++ b/solution.py
@@ -177,7 +177,7 @@
         slot_match = jnp.arange(splits_total) == split_slot
         collected = collected + jnp.where(slot_match[:, None, None], child_pair[None], 0.0)
         slot_list.append(split_slot)
-    totals = lax.psum(collected, ("rows", "feat"))
+    totals = jnp.sum(lax.all_gather(collected, ("rows", "feat")), axis=0)
     child_scores = jnp.stack([totals[slot_index] for slot_index in slot_list], 0)[:, None]
     return (gain_list[0], gain_list[1], gain_list[2], child_scores)
 

time: 718 us -> 771 us (1.074)
  waiting for transfers between devices: 148 us -> 260 us
  blocking collectives: 76.1 us -> 0 us
  between operations: 13.7 us -> 27.2 us
    all_gather x0 -> x1, waiting for transfers between devices: none -> 112 us  [on_device(): totals = jnp.sum(lax.all_gather(collected, ('rows', 'feat')), axis=0)]
    psum x1 -> x0, blocking collectives: 76.1 us -> none  [on_device(): totals = lax.psum(collected, ('rows', 'feat'))]
  transfers between devices with their start and end apart: 35 -> 36, of which waited for: 14 -> 15; matrix products, arithmetic and copies ran while one was open for 52% -> 48% of each run, Pallas kernels for 0% -> 0%
where the time goes in v1:
time: 771 us; the launch traced here: 761 us
  local copies, waits for them, and re-layouts  310 us (40%)
  waiting for transfers between devices  260 us (34%)
  starting transfers between devices  69.2 us (9%)
  other arithmetic  61.7 us (8%)
  matrix products  30.3 us (4%)
  between operations  27.2 us (4%)
    gather x36, local copies, waits for them, and re-layouts, front_index(): source = jnp.searchsorted(running, wanted, side='left')  222 us
    ppermute x35, waiting for transfers between devices, swapped(): return lax.ppermute(block, axis, route)  148 us
    all_gather x1, waiting for transfers between devices, on_device(): totals = jnp.sum(lax.all_gather(collected, ('rows', 'feat')), axis=0)  112 us
    ppermute x35, starting transfers between devices, swapped(): return lax.ppermute(block, axis, route)  69.2 us
    dot_general x12, matrix products, add_block(): jnp.dot(one_hot, grad_block, preferred_element_type=jnp.float32)  22.6 us
    gather x3, local copies, waits for them, and re-layouts, pick_slots(): taken = jnp.take(values, source, axis=0)  20.4 us
    gather x5, local copies, waits for them, and re-layouts, pick_columns(): taken = jnp.take(values, source, axis=1)  19 us
  transfers between devices with their start and end apart: 36, of which 15 were waited for; matrix products, arithmetic and copies ran while one was open for 48% of the time, Pallas kernels for 0%

profile of v1, /device:TPU:1, one launch (start us, length us, event | category | flops | bytes accessed | tf_op | source)
XLA Modules:
  0.0 760.7 jit_solution(2612169343144147408)
XLA Ops:
  8.7 3.7 collective-permute-start
  28.6 74.8 %while.98 = (s32[]{:T(128)}, u32[1024]{0:T(1024)S(1)}, u32[1024]{0:T(1024)S(1)}, s32[2048]{0:T(1024)S(1)}, s32[]{:T(128)}, /*index=5*/s32[]{:T(128)}, s32[]{}) while((s32[]{:T(128)}, u32[1024]{0:T(1024)S(1)}, u32[1024]{0:T(1024)S(1)}, s32[2048]{0:T(1024)S(1)}, s32[]{:T(128)}, /*index=5*/s32[]{:T(128)}, s32[]{}) %tuple.223), condition=%wide.region_3.4_spmd.clone, body=%wide.region_2.3_spmd.clone.sunk | while | flops 20484 | bytes 63589 | solution.py:49
  28.6 6.2 gather_fusion
  34.8 6.2 gather_fusion
  41.1 6.2 gather_fusion
  47.3 6.2 gather_fusion
  53.5 6.2 gather_fusion
  59.8 6.2 gather_fusion
  66.0 6.2 gather_fusion
  72.2 6.2 gather_fusion
  78.5 6.2 gather_fusion
  84.7 6.2 gather_fusion
  90.9 6.2 gather_fusion
  97.2 6.2 gather_fusion
  104.1 6.8 gather_fusion.5
  118.8 74.8 %while.100 = (s32[]{:T(128)}, u32[1024]{0:T(1024)S(1)}, u32[1024]{0:T(1024)S(1)}, s32[2048]{0:T(1024)S(1)}, s32[]{:T(128)}, /*index=5*/s32[]{:T(128)}, s32[]{}) while((s32[]{:T(128)}, u32[1024]{0:T(1024)S(1)}, u32[1024]{0:T(1024)S(1)}, s32[2048]{0:T(1024)S(1)}, s32[]{:T(128)}, /*index=5*/s32[]{:T(128)}, s32[]{}) %tuple.226), condition=%wide.region_14.19_spmd.clone, body=%wide.region_13.18_spmd.clone.sunk | while | flops 20484 | bytes 63589 | solution.py:49
  118.8 6.2 gather_fusion.1
  125.1 6.2 gather_fusion.1
  131.3 6.2 gather_fusion.1
  137.5 6.2 gather_fusion.1
  143.8 6.2 gather_fusion.1
  150.0 6.2 gather_fusion.1
  156.2 6.2 gather_fusion.1
  162.5 6.2 gather_fusion.1
  168.7 6.2 gather_fusion.1
  174.9 6.2 gather_fusion.1
  181.2 6.2 gather_fusion.1
  187.4 6.2 gather_fusion.1
  194.9 6.8 gather_fusion.9
  206.2 7.0 collective-permute-start.26
  217.4 74.8 %while.102 = (s32[]{:T(128)}, u32[1024]{0:T(1024)S(1)}, u32[1024]{0:T(1024)S(1)}, s32[2048]{0:T(1024)S(1)}, s32[]{:T(128)}, /*index=5*/s32[]{:T(128)}, s32[]{}) while((s32[]{:T(128)}, u32[1024]{0:T(1024)S(1)}, u32[1024]{0:T(1024)S(1)}, s32[2048]{0:T(1024)S(1)}, s32[]{:T(128)}, /*index=5*/s32[]{:T(128)}, s32[]{}) %tuple.229), condition=%wide.region_25.30_spmd.clone, body=%wide.region_24.29_spmd.clone.sunk | while | flops 20484 | bytes 63589 | solution.py:49
  217.4 6.2 gather_fusion.2
  223.6 6.2 gather_fusion.2
  229.9 6.2 gather_fusion.2
  236.1 6.2 gather_fusion.2
  242.3 6.2 gather_fusion.2
  248.6 6.2 gather_fusion.2
  254.8 6.2 gather_fusion.2
  261.0 6.2 gather_fusion.2
  267.3 6.2 gather_fusion.2
  273.5 6.2 gather_fusion.2
  279.7 6.2 gather_fusion.2
  286.0 6.2 gather_fusion.2
  292.8 6.8 gather_fusion.13
  300.0 4.0 gather_fusion.3
  309.8 6.0 collective-permute-done.15
  317.9 4.1 gather_fusion.7
  326.9 4.3 gather_fusion.4
  332.5 10.0 %collective-permute-done.27 = s32[32,1024]{0,1:T(8,128)} collective-permute-done((s32[32,1024]{0,1:T(8,128)S(1)}, s32[32,1024]{0,1:T(8,128)}, u32[]{:S(2)}, u32[]{:S(2)}) %collective-permute-start.27) | collective-permute-done | bytes 131104 | tf_op jit(solution)/shard_map/ppermute | solution.py:24
  344.6 5.3 gather_fusion.11
  354.3 14.4 %while.99 = (s32[]{:T(128)}, f32[4096,128]{1,0:T(8,128)S(1)}, f32[4096]{0:T(1024)S(1)}, s32[64,1024]{1,0:T(8,128)}, bf16[1024,128]{1,0:T(8,128)(2,1)S(1)}, /*ind...) while((s32[]{:T(128)}, f32[4096,128]{1,0:T(8,128)S(1)}, ...), condition=%wide.region_5.9_spmd.clone, body=%wide.region_4.8_spmd.clone.sunk | while | flops 272637952 | bytes 7735978 | solution.py:89
  377.9 8.6 %collective-permute-start.10 = (f32[8,64]{1,0:T(8,128)S(1)}, f32[8,64]{1,0:T(8,128)S(1)}, u32[]{:S(2)}, u32[]{:S(2)}) collective-permute-start(f32[8,64]{1,0:T(8,128)S(1)} %slice_select_fusion.26), channel_id=1, source_target_pairs={{0,16},{16,0},{4,20},{20,4},{8,24},{24,8},{12,28},{28,12},{32,48},... | collective-permute-start | bytes 6152 | tf_op jit(solution)/shard_map/ppermute | solution.py:24
  401.8 22.7 %while.101 = (s32[]{:T(128)}, f32[4096,128]{1,0:T(8,128)}, f32[4096]{0:T(1024)S(1)}, s32[64,1024]{1,0:T(8,128)}, bf16[1024,128]{1,0:T(8,128)(2,1)S(1)}, /*index=...) while((s32[]{:T(128)}, f32[4096,128]{1,0:T(8,128)}, ...), condition=%wide.region_16.21_spmd.clone, body=%wide.region_15.20_spmd.clone.sunk | while | flops 272637952 | bytes 7735978 | solution.py:89
  408.0 3.7 convolution_add_fusion.7
  426.8 6.4 collective-permute-start.12
  455.1 17.1 %while.103 = (s32[]{:T(128)}, f32[4096,128]{1,0:T(8,128)S(1)}, f32[4096]{0:T(1024)S(1)}, s32[64,1024]{1,0:T(8,128)}, bf16[1024,128]{1,0:T(8,128)(2,1)S(1)}, /*in...) while((s32[]{:T(128)}, f32[4096,128]{1,0:T(8,128)S(1)}, ...), condition=%wide.region_27.32_spmd.clone, body=%wide.region_26.31_spmd.clone.sunk | while | flops 272637952 | bytes 7735978 | solution.py:89
  472.4 7.1 collective-permute-start.24
  479.5 18.7 %collective-permute-done.32 = f32[32,64]{1,0:T(8,128)S(1)} collective-permute-done((f32[32,64]{1,0:T(8,128)S(1)}, f32[32,64]{1,0:T(8,128)S(1)}, u32[]{:S(2)}, u32[]{:S(2)}) %collective-permute-start.32) | collective-permute-done | bytes 8224 | tf_op jit(solution)/shard_map/ppermute | solution.py:24
  514.9 73.3 %collective-permute-done.29 = f32[32,8192]{1,0:T(8,128)} collective-permute-done((f32[32,8192]{1,0:T(8,128)}, f32[32,8192]{1,0:T(8,128)}, u32[]{:S(2)}, u32[]{:S(2)}) %collective-permute-start.29) | collective-permute-done | bytes 1048608 | tf_op jit(solution)/shard_map/ppermute | solution.py:24
  591.8 7.6 collective-permute-done.18
  599.5 11.2 %collective-permute-done.5 = f32[8,8192]{1,0:T(8,128)S(1)} collective-permute-done((f32[8,8192]{1,0:T(8,128)S(1)}, f32[8,8192]{1,0:T(8,128)S(1)}, u32[]{:S(2)}, u32[]{:S(2)}) %collective-permute-start.5) | collective-permute-done | bytes 262176 | tf_op jit(solution)/shard_map/ppermute | solution.py:24
  612.7 6.3 collective-permute-done.6
  619.7 4.9 collective-permute-done.19
  637.2 112.5 %all-gather.2.cloned.1.call-done = f32[256,14,2,128]{3,2,1,0:T(2,128)} async-done(((f32[1,14,2,128]{3,2,1,0:T(2,128)}), f32[256,14,2,128]{3,2,1,0:T(2,128)}) %all-gather.2.cloned.1.call-update) | async-done | bytes 3670032 | tf_op jit(solution)/shard_map/all_gather | solution.py:180
  (559 shorter events, 185.0 us)
Async XLA Ops:
  7.2 742.6 %all-gather.2.cloned.1.call-start = ((), (), s32[]{:S(2)}) async-start(), calls=%async_computation | async-start | bytes 3684352 | tf_op jit(solution)/shard_map/all_gather | solution.py:180
  8.7 18.7 %collective-permute-start = (bf16[1024]{0:T(1024)(128)(2,1)S(1)}, bf16[1024]{0:T(1024)(128)(2,1)S(1)}, u32[]{:S(2)}, u32[]{:S(2)}) collective-permute-start(bf16[1024]{0:T(1024)(128)(2,1)S(1)} %and_select_fusion.2), channel_id=1, source_target_pairs={{0,128},{128,0},{4,132},{132,4},{8,136},{136,8},{12,140},{140,12},... | collective-permute-start | bytes 6152 | tf_op jit(solution)/shard_map/ppermute | solution.py:24
  13.1 97.8 %collective-permute-start.13 = (s32[3,1024]{1,0:T(4,128)S(1)}, s32[3,1024]{1,0:T(4,128)S(1)}, u32[]{:S(2)}, u32[]{:S(2)}) collective-permute-start(s32[3,1024]{1,0:T(4,128)S(1)} %concatenate.74), channel_id=1, source_target_pairs={{0,128},{128,0},{4,132},{132,4},{8,136},{136,8},{12,140},{140,12},... | collective-permute-start | bytes 36872 | tf_op jit(solution)/shard_map/ppermute | solution.py:24
  14.0 285.6 %collective-permute-start.1 = (s32[32,1024]{1,0:T(8,128)S(1)}, s32[32,1024]{1,0:T(8,128)S(1)}, u32[]{:S(2)}, u32[]{:S(2)}) collective-permute-start(s32[32,1024]{1,0:T(8,128)S(1)} %concatenate.78), channel_id=1, source_target_pairs={{0,128},{128,0},{4,132},{132,4},{8,136},{136,8},{12,140},{140,12},... | collective-permute-start | bytes 393224 | tf_op jit(solution)/shard_map/ppermute | solution.py:24
  18.7 306.9 %collective-permute-start.2 = (bf16[1024,128]{1,0:T(8,128)(2,1)}, bf16[1024,128]{1,0:T(8,128)(2,1)}, u32[]{:S(2)}, u32[]{:S(2)}) collective-permute-start(bf16[1024,128]{1,0:T(8,128)(2,1)} %concatenate.80), channel_id=1, source_target_pairs={{0,128},{128,0},{4,132},{132,4},{8,136},{136,8},{12,140},{140,12},... | collective-permute-start | bytes 786440 | tf_op jit(solution)/shard_map/ppermute | solution.py:24
  28.6 75.5 %copy-start.8 = (bf16[512]{0:T(512)(128)(2,1)S(1)}, bf16[512]{0:T(512)(128)(2,1)}, u32[]{:S(2)}) copy-start(bf16[512]{0:T(512)(128)(2,1)} %param.27) | copy-start | bytes 3076
  103.4 7.5 copy-start.7
  115.7 2.5 collective-permute-start.14
  117.7 84.0 %collective-permute-start.25 = (s32[3,1024]{0,1:T(8,128)S(1)}, s32[3,1024]{0,1:T(8,128)S(1)}, u32[]{:S(2)}, u32[]{:S(2)}) collective-permute-start(s32[3,1024]{0,1:T(8,128)S(1)} %bitcast_select_fusion.2), channel_id=1, source_target_pairs={{0,64},{64,0},{4,68},{68,4},{8,72},{72,8},{12,76},{76,12},{16,80},... | collective-permute-start | bytes 36872 | tf_op jit(solution)/shard_map/ppermute | solution.py:24
  206.2 10.6 %collective-permute-start.26 = (bf16[1024]{0:T(1024)(128)(2,1)S(1)}, bf16[1024]{0:T(1024)(128)(2,1)S(1)}, u32[]{:S(2)}, u32[]{:S(2)}) collective-permute-start(bf16[1024]{0:T(1024)(128)(2,1)S(1)} %and_select_fusion), channel_id=1, source_target_pairs={{0,32},{32,0},{4,36},{36,4},{8,40},{40,8},{12,44},{44,12},{16,48},... | collective-permute-start | bytes 6152 | tf_op jit(solution)/shard_map/ppermute | solution.py:24
  292.2 7.4 copy-start.6
  305.4 10.4 %collective-permute-start.15 = (s32[32,1024]{0,1:T(8,128)S(1)}, s32[32,1024]{0,1:T(8,128)}, u32[]{:S(2)}, u32[]{:S(2)}) collective-permute-start(s32[32,1024]{0,1:T(8,128)S(1)} %bitcast_select_fusion.3), channel_id=1, source_target_pairs={{0,64},{64,0},{4,68},{68,4},{8,72},{72,8},{12,76},{76,12},{16,80},... | collective-permute-start | bytes 393224 | tf_op jit(solution)/shard_map/ppermute | solution.py:24
  308.6 41.2 %copy-start.9 = (pred[1024]{0:T(1024)(128)(4,1)}, pred[1024]{0:T(1024)(128)(4,1)S(1)}, u32[]{:S(2)}) copy-start(pred[1024]{0:T(1024)(128)(4,1)S(1)} %fusion.26) | copy-start | bytes 3076
  317.9 7.7 %copy-start.5 = (bf16[512,128]{1,0:T(8,128)(2,1)S(1)}, bf16[512,128]{1,0:T(8,128)(2,1)}, u32[]{:S(2)}) copy-start(bf16[512,128]{1,0:T(8,128)(2,1)} %param.26) | copy-start | bytes 393220
  322.3 20.2 %collective-permute-start.27 = (s32[32,1024]{0,1:T(8,128)S(1)}, s32[32,1024]{0,1:T(8,128)}, u32[]{:S(2)}, u32[]{:S(2)}) collective-permute-start(s32[32,1024]{0,1:T(8,128)S(1)} %bitcast_select_fusion.1), channel_id=1, source_target_pairs={{0,32},{32,0},{4,36},{36,4},{8,40},{40,8},{12,44},{44,12},{16,48},... | collective-permute-start | bytes 393224 | tf_op jit(solution)/shard_map/ppermute | solution.py:24
  344.6 8.7 %copy-start.3 = (s32[64,1024]{1,0:T(8,128)S(1)}, s32[64,1024]{1,0:T(8,128)}, u32[]{:S(2)}) copy-start(s32[64,1024]{1,0:T(8,128)} %shift_right_arithmetic.97) | copy-start | bytes 786436
  344.6 8.7 %copy-start.4 = (s32[64,1024]{1,0:T(8,128)S(1)}, s32[64,1024]{1,0:T(8,128)}, u32[]{:S(2)}) copy-start(s32[64,1024]{1,0:T(8,128)} %shift_right_arithmetic.103) | copy-start | bytes 786436
  344.6 8.7 %copy-start.11 = (s32[64]{0:T(128)S(1)}, s32[64]{0:T(128)}, u32[]{:S(2)}) copy-start(s32[64]{0:T(128)} %shift_right_arithmetic.99) | copy-start | bytes 772
  368.7 5.9 copy-start
  368.8 2.6 collective-permute-start.8
  371.4 6.5 collective-permute-start.9
  377.9 9.9 %collective-permute-start.10 = (f32[8,64]{1,0:T(8,128)S(1)}, f32[8,64]{1,0:T(8,128)S(1)}, u32[]{:S(2)}, u32[]{:S(2)}) collective-permute-start(f32[8,64]{1,0:T(8,128)S(1)} %slice_select_fusion.26), channel_id=1, source_target_pairs={{0,16},{16,0},{4,20},{20,4},{8,24},{24,8},{12,28},{28,12},{32,48},... | collective-permute-start | bytes 6152 | tf_op jit(solution)/shard_map/ppermute | solution.py:24
  386.5 10.8 %collective-permute-start.16 = (bf16[1024,128]{1,0:T(8,128)(2,1)S(1)}, bf16[1024,128]{1,0:T(8,128)(2,1)}, u32[]{:S(2)}, u32[]{:S(2)}) collective-permute-start(bf16[1024,128]{1,0:T(8,128)(2,1)S(1)} %get-tuple-element.1189), channel_id=1, source_target_pairs={{0,64},{64,0},{4,68},{68,4},{8,72},{72,8},{12,76},{76,12},{16,80},... | collective-permute-start | bytes 786440 | tf_op jit(solution)/shard_map/ppermute | solution.py:24
  387.8 9.5 %collective-permute-start.11 = (f32[4,64]{1,0:T(4,128)S(1)}, f32[4,64]{1,0:T(4,128)S(1)}, u32[]{:S(2)}, u32[]{:S(2)}) collective-permute-start(f32[4,64]{1,0:T(4,128)S(1)} %slice_select_fusion.28), channel_id=1, source_target_pairs={{0,8},{8,0},{4,12},{12,4},{16,24},{24,16},{20,28},{28,20},{32,40},... | collective-permute-start | bytes 3080 | tf_op jit(solution)/shard_map/ppermute | solution.py:24
  394.8 112.1 %collective-permute-start.3 = (f32[32,8192]{1,0:T(8,128)}, f32[32,8192]{1,0:T(8,128)}, u32[]{:S(2)}, u32[]{:S(2)}) collective-permute-start(f32[32,8192]{1,0:T(8,128)} %select_n.572), channel_id=1, source_target_pairs={{0,64},{64,0},{4,68},{68,4},{8,72},{72,8},{12,76},{76,12},{16,80},... | collective-permute-start | bytes 3145736 | tf_op jit(solution)/shard_map/ppermute | solution.py:24
  424.7 8.6 %collective-permute-start.21 = (f32[32,64]{1,0:T(8,128)S(1)}, f32[32,64]{1,0:T(8,128)S(1)}, u32[]{:S(2)}, u32[]{:S(2)}) collective-permute-start(f32[32,64]{1,0:T(8,128)S(1)} %select_n.624), channel_id=1, source_target_pairs={{0,32},{32,0},{4,36},{36,4},{8,40},{40,8},{12,44},{44,12},{16,48},... | collective-permute-start | bytes 24584 | tf_op jit(solution)/shard_map/ppermute | solution.py:24
  426.8 7.2 collective-permute-start.12
  433.3 4.5 collective-permute-start.22
  434.3 16.2 %collective-permute-start.28 = (bf16[1024,128]{1,0:T(8,128)(2,1)S(1)}, bf16[1024,128]{1,0:T(8,128)(2,1)}, u32[]{:S(2)}, u32[]{:S(2)}) collective-permute-start(bf16[1024,128]{1,0:T(8,128)(2,1)S(1)} %get-tuple-element.1191), channel_id=1, source_target_pairs={{0,32},{32,0},{4,36},{36,4},{8,40},{40,8},{12,44},{44,12},{16,48},... | collective-permute-start | bytes 786440 | tf_op jit(solution)/shard_map/ppermute | solution.py:24
  437.8 12.7 %collective-permute-start.23 = (f32[8,64]{1,0:T(8,128)S(1)}, f32[8,64]{1,0:T(8,128)S(1)}, u32[]{:S(2)}, u32[]{:S(2)}) collective-permute-start(f32[8,64]{1,0:T(8,128)S(1)} %slice_select_fusion.25), channel_id=1, source_target_pairs={{0,8},{8,0},{4,12},{12,4},{16,24},{24,16},{20,28},{28,20},{32,40},... | collective-permute-start | bytes 6152 | tf_op jit(solution)/shard_map/ppermute | solution.py:24
  444.2 67.3 %collective-permute-start.17 = (f32[32,8192]{1,0:T(8,128)}, f32[32,8192]{1,0:T(8,128)}, u32[]{:S(2)}, u32[]{:S(2)}) collective-permute-start(f32[32,8192]{1,0:T(8,128)} %select_n.610), channel_id=1, source_target_pairs={{0,32},{32,0},{4,36},{36,4},{8,40},{40,8},{12,44},{44,12},{16,48},... | collective-permute-start | bytes 3145736 | tf_op jit(solution)/shard_map/ppermute | solution.py:24
  447.4 7.4 copy-start.10
  472.3 26.0 %collective-permute-start.32 = (f32[32,64]{1,0:T(8,128)S(1)}, f32[32,64]{1,0:T(8,128)S(1)}, u32[]{:S(2)}, u32[]{:S(2)}) collective-permute-start(f32[32,64]{1,0:T(8,128)S(1)} %select_n.653), channel_id=1, source_target_pairs={{0,16},{16,0},{4,20},{20,4},{8,24},{24,8},{12,28},{28,12},{32,48},... | collective-permute-start | bytes 24584 | tf_op jit(solution)/shard_map/ppermute | solution.py:24
  472.4 26.0 %collective-permute-start.24 = (f32[4,64]{1,0:T(4,128)S(1)}, f32[4,64]{1,0:T(4,128)S(1)}, u32[]{:S(2)}, u32[]{:S(2)}) collective-permute-start(f32[4,64]{1,0:T(4,128)S(1)} %slice_select_fusion.27), channel_id=1, source_target_pairs={{0,4},{4,0},{8,12},{12,8},{16,20},{20,16},{24,28},{28,24},{32,36},... | collective-permute-start | bytes 3080 | tf_op jit(solution)/shard_map/ppermute | solution.py:24
  498.3 2.6 collective-permute-start.33
  500.9 5.8 collective-permute-start.34
  503.5 3.4 copy-start.1
  506.0 82.2 %collective-permute-start.29 = (f32[32,8192]{1,0:T(8,128)}, f32[32,8192]{1,0:T(8,128)}, u32[]{:S(2)}, u32[]{:S(2)}) collective-permute-start(f32[32,8192]{1,0:T(8,128)} %select_n.642), channel_id=1, source_target_pairs={{0,16},{16,0},{4,20},{20,4},{8,24},{24,8},{12,28},{28,12},{32,48},... | collective-permute-start | bytes 3145736 | tf_op jit(solution)/shard_map/ppermute | solution.py:24
  506.9 4.7 copy-start.2
  508.4 81.4 %collective-permute-start.4 = (f32[16,8192]{1,0:T(8,128)S(1)}, f32[16,8192]{1,0:T(8,128)S(1)}, u32[]{:S(2)}, u32[]{:S(2)}) collective-permute-start(f32[16,8192]{1,0:T(8,128)S(1)} %slice_select_fusion.9), channel_id=1, source_target_pairs={{0,32},{32,0},{4,36},{36,4},{8,40},{40,8},{12,44},{44,12},{16,48},... | collective-permute-start | bytes 1572872 | tf_op jit(solution)/shard_map/ppermute | solution.py:24
  513.0 86.4 %collective-permute-start.18 = (f32[16,8192]{1,0:T(8,128)S(1)}, f32[16,8192]{1,0:T(8,128)S(1)}, u32[]{:S(2)}, u32[]{:S(2)}) collective-permute-start(f32[16,8192]{1,0:T(8,128)S(1)} %slice_select_fusion.8), channel_id=1, source_target_pairs={{0,16},{16,0},{4,20},{20,4},{8,24},{24,8},{12,28},{28,12},{32,48},... | collective-permute-start | bytes 1572872 | tf_op jit(solution)/shard_map/ppermute | solution.py:24
  589.6 35.7 %collective-permute-start.30 = (f32[16,8192]{1,0:T(8,128)S(1)}, f32[16,8192]{1,0:T(8,128)S(1)}, u32[]{:S(2)}, u32[]{:S(2)}) collective-permute-start(f32[16,8192]{1,0:T(8,128)S(1)} %slice_select_fusion.7), channel_id=1, source_target_pairs={{0,8},{8,0},{4,12},{12,4},{16,24},{24,16},{20,28},{28,20},{32,40},... | collective-permute-start | bytes 1572872 | tf_op jit(solution)/shard_map/ppermute | solution.py:24
  589.8 20.8 %collective-permute-start.5 = (f32[8,8192]{1,0:T(8,128)S(1)}, f32[8,8192]{1,0:T(8,128)S(1)}, u32[]{:S(2)}, u32[]{:S(2)}) collective-permute-start(f32[8,8192]{1,0:T(8,128)S(1)} %slice_select_fusion.12), channel_id=1, source_target_pairs={{0,16},{16,0},{4,20},{20,4},{8,24},{24,8},{12,28},{28,12},{32,48},... | collective-permute-start | bytes 786440 | tf_op jit(solution)/shard_map/ppermute | solution.py:24
  610.8 8.2 %collective-permute-start.6 = (f32[4,8192]{1,0:T(4,128)S(1)}, f32[4,8192]{1,0:T(4,128)S(1)}, u32[]{:S(2)}, u32[]{:S(2)}) collective-permute-start(f32[4,8192]{1,0:T(4,128)S(1)} %slice_select_fusion.14), channel_id=1, source_target_pairs={{0,8},{8,0},{4,12},{12,4},{16,24},{24,16},{20,28},{28,20},{32,40},... | collective-permute-start | bytes 393224 | tf_op jit(solution)/shard_map/ppermute | solution.py:24
  611.2 13.4 %collective-permute-start.19 = (f32[8,8192]{1,0:T(8,128)S(1)}, f32[8,8192]{1,0:T(8,128)S(1)}, u32[]{:S(2)}, u32[]{:S(2)}) collective-permute-start(f32[8,8192]{1,0:T(8,128)S(1)} %slice_select_fusion.11), channel_id=1, source_target_pairs={{0,8},{8,0},{4,12},{12,4},{16,24},{24,16},{20,28},{28,20},{32,40},... | collective-permute-start | bytes 786440 | tf_op jit(solution)/shard_map/ppermute | solution.py:24
  619.1 6.5 collective-permute-start.7
  624.6 1.5 copy-start.15
  624.6 1.5 copy-start.16
  624.7 4.3 copy-start.19
  624.7 4.3 copy-start.20
  624.7 3.7 collective-permute-start.20
  625.4 6.5 copy-start.17
  625.4 6.5 copy-start.18
  625.4 9.0 %copy-start.12 = (pred[14]{0:T(512)(128)(4,1)S(1)}, pred[14]{0:T(512)(128)(4,1)}, u32[]{:S(2)}) copy-start(pred[14]{0:T(512)(128)(4,1)} %get-tuple-element.829) | copy-start | bytes 46
  625.4 9.0 %copy-start.13 = (pred[14]{0:T(512)(128)(4,1)S(1)}, pred[14]{0:T(512)(128)(4,1)}, u32[]{:S(2)}) copy-start(pred[14]{0:T(512)(128)(4,1)} %get-tuple-element.830) | copy-start | bytes 46
  625.4 9.0 %copy-start.14 = (pred[14]{0:T(512)(128)(4,1)S(1)}, pred[14]{0:T(512)(128)(4,1)}, u32[]{:S(2)}) copy-start(pred[14]{0:T(512)(128)(4,1)} %iota_compare_fusion.2) | copy-start | bytes 46
  625.4 5.9 collective-permute-start.31
Sparse Core Ops, SparseCore 0:
  635.2 114.4 all-gather.1
